TPU v7x, 32 devices: a whole 2x2x4 slice. The times are simulated.
32 devices in a mesh: dom: 4 (over y, x), freq: 8 (over z, core).
Axes of the slice: x: 2, y: 2, z: 4, core: 2. Of those that a mesh axis runs over, the one named last changes fastest.
Arguments:
- voltages: float32 [512, 8192], P('freq', 'dom'), may hold values from -5 to 5
- sources: float32 [512, 8192], P('freq', 'dom'), may hold values from -20 to 20
- terminals: int32 [2, 16384], P(None, 'dom'), may hold values from 0 to 2559, as said below
- elem_current: float32 [2, 16384], P(None, 'dom'), may hold values from 0.2 to 2
- elem_charge: float32 [2, 16384], P(None, 'dom'), may hold values from 0.1 to 1
- jacobi: float32 [256, 2, 2, 8192], P('freq', None, None, 'dom'), may hold values from -1.2 to 2
Outputs:
- residual: float32 [512, 8192], P('freq', 'dom')
- newton_step: float32 [512, 8192], P('freq', 'dom')
- residual_norm: float32 [], replicated
Inputs may be any that keep to these rules, and one draw needn't show every extreme that they name: `terminals`: A terminal value below 2048 is a node of the element's own partition; a value v of 2048 or more is node (v - 2048) % 128 of partition (v - 2048) // 128, one of that partition's first 128 nodes.
All inputs are finite; a program needn't handle non-finite values.
Results may differ from a plain program's by a relative error of at most 0.0003.
Values sent between devices are 32-bit elements; how exact they have to be, the bound alone decides.
A program may use at most 64 MiB of HBM per device.

v0:
```python
import math

import jax
import jax.numpy as jnp
from jax import lax
from jax.sharding import PartitionSpec as P

S = 512


trust_radius = 2.0


def transform_table(samples):
    row_index = jnp.arange(samples, dtype=jnp.int32)
    harmonic = row_index // 2
    is_sine = row_index % 2 == 1
    column = jnp.arange(samples, dtype=jnp.int32)
    order = jnp.where(harmonic == 0, jnp.where(is_sine, samples // 2, 0), harmonic)
    phase = (order[:, None] * column[None, :] % samples).astype(jnp.float32) * (
        2.0 * math.pi / samples
    )
    use_sine = is_sine & (harmonic > 0)
    values = jnp.where(use_sine[:, None], jnp.sin(phase), jnp.cos(phase))
    weight = jnp.where(harmonic == 0, math.sqrt(1.0 / samples), math.sqrt(2.0 / samples)).astype(
        jnp.float32
    )
    forward = values * weight[:, None]
    pairs = forward.reshape(samples // 2, 2, samples)
    rate = 2.0 / samples * jnp.arange(samples // 2, dtype=jnp.float32)
    derived = jnp.stack([pairs[:, 1], -pairs[:, 0]], axis=1) * rate[:, None, None]
    return jnp.concatenate([forward, derived.reshape(samples, samples)], axis=1)


def incidence_sum(flows, terminals, column_count):
    flow_rows = flows.shape[0]
    elem_count = flows.shape[1]
    block_size = math.gcd(elem_count, 512)
    block_count = elem_count // block_size
    flow_blocks = flows.reshape(flow_rows, block_count, block_size).transpose(1, 0, 2)
    term_blocks = terminals.reshape(2, block_count, block_size).transpose(1, 0, 2)
    columns = jnp.arange(column_count, dtype=jnp.int32)

    def accumulate(total, pieces):
        flow_piece, term_piece = pieces
        plus = (term_piece[0][:, None] == columns[None, :]).astype(jnp.float32)
        minus = (term_piece[1][:, None] == columns[None, :]).astype(jnp.float32)
        signed = plus - minus
        total = total + jnp.dot(
            flow_piece, signed, precision=lax.Precision.HIGHEST, preferred_element_type=jnp.float32
        )
        return (total, None)

    start = jnp.zeros((flow_rows, column_count), jnp.float32)
    total, unused = lax.scan(accumulate, start, (flow_blocks, term_blocks))
    return total


def body(voltages, sources, terminals, elem_current, elem_charge, jacobi):
    sample_rows, node_count = voltages.shape
    freq_count = lax.axis_size("freq")
    border_count = node_count // 16
    border = lax.all_gather(voltages[:, :border_count], "dom", axis=1, tiled=True)
    extended = jnp.concatenate([voltages, border], axis=1)
    across = extended[:, terminals[0]] - extended[:, terminals[1]]
    current = elem_current[0][None, :] * across + elem_current[1][None, :] * jnp.tanh(2.0 * across)
    charge = elem_charge[0][None, :] * across + elem_charge[1][None, :] * jnp.tanh(across)
    flows = jnp.concatenate([current, charge], axis=0)
    totals = incidence_sum(flows, terminals, extended.shape[1]).reshape(
        2, sample_rows, extended.shape[1]
    )
    incoming = lax.psum_scatter(totals[:, :, node_count:], "dom", scatter_dimension=2, tiled=True)
    owned = totals[:, :, :node_count]
    owned = jnp.concatenate(
        [owned[:, :, :border_count] + incoming, owned[:, :, border_count:]], axis=2
    )
    table = transform_table(S)
    node_block = node_count // freq_count
    grouped = owned.reshape(2, sample_rows, freq_count, node_block)
    block = lax.all_to_all(grouped, "freq", split_axis=2, concat_axis=1, tiled=True)
    flat = block.reshape(2 * S, block.shape[3])
    spectra = jnp.dot(
        table, flat, precision=lax.Precision.HIGHEST, preferred_element_type=jnp.float32
    )
    transformed = lax.all_to_all(spectra, "freq", split_axis=0, concat_axis=1, tiled=True)
    residual = transformed - sources
    pairs = residual.reshape(sample_rows // 2, 2, node_count)
    raw = -(jacobi[:, :, 0, :] * pairs[:, 0:1, :] + jacobi[:, :, 1, :] * pairs[:, 1:2, :])
    raw = raw.reshape(sample_rows, node_count)
    step_squares, residual_squares = lax.psum(
        (jnp.sum(raw * raw), jnp.sum(residual * residual)), ("dom", "freq")
    )
    entry_count = S * node_count * lax.axis_size("dom")
    spread = jnp.sqrt(step_squares / entry_count + 1e-06)
    newton_step = raw * jnp.minimum(1.0, trust_radius / spread)
    residual_norm = jnp.sqrt(residual_squares)
    return (residual, newton_step, residual_norm)


def solution(mesh):
    placed = (
        P("freq", "dom"),
        P("freq", "dom"),
        P(None, "dom"),
        P(None, "dom"),
        P(None, "dom"),
        P("freq", None, None, "dom"),
    )
    return jax.shard_map(
        body,
        mesh=mesh,
        in_specs=placed,
        out_specs=(P("freq", "dom"), P("freq", "dom"), P()),
        check_vma=False,
    )
```

profile of v0, /device:TPU:0, one launch (start us, length us, event | category | flops | bytes accessed | tf_op | source)
XLA Modules:
  0.0 226.1 jit_solution(1652507804169828235)
XLA Ops:
  7.2 1.4 copy.26
  8.6 10.5 %all_gather.3 = f32[64,512]{0,1:T(8,128)S(1)} all-gather(f32[64,128]{0,1:T(8,128)S(1)} %slice.85), channel_id=1, replica_groups=mesh['dom'=4,'freq'=8] {'dom'}, dimensions={1}, use_global_device_ids=true | all-gather | bytes 163840 | tf_op jit(solution)/shard_map/all_gather | solution.py:63
  19.3 14.1 %gather_fusion = f32[4096,64]{1,0:T(8,128)} fusion(f32[64,2560]{0,1:T(8,128)S(1)} %pad_maximum_fusion, s32[4096]{0:T(1024)S(1)} %broadcast_clamp_fusion.1), kind=kCustom, calls=%fused_computation | custom fusion | bytes 2113536 | tf_op jit(solution)/shard_map/gather | solution.py:65
  33.4 14.1 %gather_fusion.1 = f32[4096,64]{1,0:T(8,128)} fusion(f32[64,2560]{0,1:T(8,128)S(1)} %pad_maximum_fusion, s32[4096]{0:T(1024)S(1)} %broadcast_clamp_fusion), kind=kCustom, calls=%fused_computation.1 | custom fusion | bytes 2113536 | tf_op jit(solution)/shard_map/gather | solution.py:65
  47.4 2.4 %sub.30 = f32[4096,64]{1,0:T(8,128)S(1)} subtract(f32[4096,64]{1,0:T(8,128)} %gather_fusion, f32[4096,64]{1,0:T(8,128)} %gather_fusion.1) | non-fusion elementwise | flops 262144 | bytes 3145728 | tf_op jit(solution)/shard_map/sub | solution.py:65
  49.9 0.6 copy.27
  50.5 0.1 copy-done.5
  50.7 0.2 slice_reduce_fusion.3
  50.9 0.3 multiply_add_fusion.1
  51.2 0.2 maximum_bitcast_fusion
  51.4 1.1 copy-done.1
  52.5 35.5 %while.12 = (s32[]{:T(128)}, f32[128,2560]{1,0:T(8,128)S(1)}, f32[8,128,512]{2,1,0:T(8,128)S(1)}, s32[8,2,512]{2,1,0:T(2,128)S(1)}, s32[]{:T(128)}, /*index=5*/s32[]{:T(128)}, s32[]{}) while((s32[]{:T(128)}, f32[128,2560]{1,0:T(8,128)S(1)}, f32[8,128,512]{2,1,0:T(8,128)S(1)}, s32[8,2,512]{2,1,0:T(2,128)S(1)}, ...), condition=%wide.region_1.2_spmd.clone.clone, body=%wide.region_0.1_spmd.clone.clone.sunk | while | flops 2020474880 | bytes 2895983 | solution.py:55
  52.5 4.4 %fusion.52 = f32[128,2560]{1,0:T(8,128)S(1)} fusion(s32[512]{0:T(512)S(1)} %bitcast.65, s32[512]{0:T(512)S(1)} %bitcast.64, f32[128,2560]{1,0:T(8,128)S(1)} %get-tuple-element.133, pred[]{:T(512)S(6)} %compare.14, f32[8,128,512]{2,1,0:T(8,128)S(1)} %get-tuple-element.141, s32[]{:T(128)} %get-tuple-element.132), kind=kOutput, calls=%fused_computation.9.clone.1 | convolution fusion | flops 2020474880 | bytes 2887685 | tf_op jit(solution)/shard_map/while/body/eval_jaxpr/dot_general | solution.py:49
  57.0 4.4 %fusion.52 = f32[128,2560]{1,0:T(8,128)S(1)} fusion(s32[512]{0:T(512)S(1)} %bitcast.65, s32[512]{0:T(512)S(1)} %bitcast.64, f32[128,2560]{1,0:T(8,128)S(1)} %get-tuple-element.133, pred[]{:T(512)S(6)} %compare.14, f32[8,128,512]{2,1,0:T(8,128)S(1)} %get-tuple-element.141, s32[]{:T(128)} %get-tuple-element.132), kind=kOutput, calls=%fused_computation.9.clone.1 | convolution fusion | flops 2020474880 | bytes 2887685 | tf_op jit(solution)/shard_map/while/body/eval_jaxpr/dot_general | solution.py:49
  61.4 4.4 %fusion.52 = f32[128,2560]{1,0:T(8,128)S(1)} fusion(s32[512]{0:T(512)S(1)} %bitcast.65, s32[512]{0:T(512)S(1)} %bitcast.64, f32[128,2560]{1,0:T(8,128)S(1)} %get-tuple-element.133, pred[]{:T(512)S(6)} %compare.14, f32[8,128,512]{2,1,0:T(8,128)S(1)} %get-tuple-element.141, s32[]{:T(128)} %get-tuple-element.132), kind=kOutput, calls=%fused_computation.9.clone.1 | convolution fusion | flops 2020474880 | bytes 2887685 | tf_op jit(solution)/shard_map/while/body/eval_jaxpr/dot_general | solution.py:49
  65.9 4.4 %fusion.52 = f32[128,2560]{1,0:T(8,128)S(1)} fusion(s32[512]{0:T(512)S(1)} %bitcast.65, s32[512]{0:T(512)S(1)} %bitcast.64, f32[128,2560]{1,0:T(8,128)S(1)} %get-tuple-element.133, pred[]{:T(512)S(6)} %compare.14, f32[8,128,512]{2,1,0:T(8,128)S(1)} %get-tuple-element.141, s32[]{:T(128)} %get-tuple-element.132), kind=kOutput, calls=%fused_computation.9.clone.1 | convolution fusion | flops 2020474880 | bytes 2887685 | tf_op jit(solution)/shard_map/while/body/eval_jaxpr/dot_general | solution.py:49
  70.3 4.4 %fusion.52 = f32[128,2560]{1,0:T(8,128)S(1)} fusion(s32[512]{0:T(512)S(1)} %bitcast.65, s32[512]{0:T(512)S(1)} %bitcast.64, f32[128,2560]{1,0:T(8,128)S(1)} %get-tuple-element.133, pred[]{:T(512)S(6)} %compare.14, f32[8,128,512]{2,1,0:T(8,128)S(1)} %get-tuple-element.141, s32[]{:T(128)} %get-tuple-element.132), kind=kOutput, calls=%fused_computation.9.clone.1 | convolution fusion | flops 2020474880 | bytes 2887685 | tf_op jit(solution)/shard_map/while/body/eval_jaxpr/dot_general | solution.py:49
  74.7 4.4 %fusion.52 = f32[128,2560]{1,0:T(8,128)S(1)} fusion(s32[512]{0:T(512)S(1)} %bitcast.65, s32[512]{0:T(512)S(1)} %bitcast.64, f32[128,2560]{1,0:T(8,128)S(1)} %get-tuple-element.133, pred[]{:T(512)S(6)} %compare.14, f32[8,128,512]{2,1,0:T(8,128)S(1)} %get-tuple-element.141, s32[]{:T(128)} %get-tuple-element.132), kind=kOutput, calls=%fused_computation.9.clone.1 | convolution fusion | flops 2020474880 | bytes 2887685 | tf_op jit(solution)/shard_map/while/body/eval_jaxpr/dot_general | solution.py:49
  79.2 4.4 %fusion.52 = f32[128,2560]{1,0:T(8,128)S(1)} fusion(s32[512]{0:T(512)S(1)} %bitcast.65, s32[512]{0:T(512)S(1)} %bitcast.64, f32[128,2560]{1,0:T(8,128)S(1)} %get-tuple-element.133, pred[]{:T(512)S(6)} %compare.14, f32[8,128,512]{2,1,0:T(8,128)S(1)} %get-tuple-element.141, s32[]{:T(128)} %get-tuple-element.132), kind=kOutput, calls=%fused_computation.9.clone.1 | convolution fusion | flops 2020474880 | bytes 2887685 | tf_op jit(solution)/shard_map/while/body/eval_jaxpr/dot_general | solution.py:49
  83.6 4.4 %fusion.52 = f32[128,2560]{1,0:T(8,128)S(1)} fusion(s32[512]{0:T(512)S(1)} %bitcast.65, s32[512]{0:T(512)S(1)} %bitcast.64, f32[128,2560]{1,0:T(8,128)S(1)} %get-tuple-element.133, pred[]{:T(512)S(6)} %compare.14, f32[8,128,512]{2,1,0:T(8,128)S(1)} %get-tuple-element.141, s32[]{:T(128)} %get-tuple-element.132), kind=kOutput, calls=%fused_computation.9.clone.1 | convolution fusion | flops 2020474880 | bytes 2887685 | tf_op jit(solution)/shard_map/while/body/eval_jaxpr/dot_general | solution.py:49
  88.0 0.7 slice.87
  88.9 0.1 fusion.34
  89.1 0.1 compare_select_fusion.3
  89.2 24.4 %reduce-scatter.2.cloned.1.call-done = f32[2,64,128]{2,1,0:T(8,128)} async-done(((f32[2,64,512]{2,1,0:T(8,128)}), f32[2,64,128]{2,1,0:T(8,128)}) %reduce-scatter.2.cloned.1.call-update) | async-done | bytes 65552 | tf_op jit(solution)/shard_map/reduce_scatter | solution.py:72
  113.6 0.9 slice_add_fusion
  114.4 0.1 pad_maximum_fusion.2
  114.5 1.1 copy.43
  115.6 4.6 %all-to-all-start = ((f32[2,64,8,256]{3,1,0,2:T(8,128)}), f32[2,64,8,256]{3,1,0,2:T(8,128)S(1)}, u32[]{:S(2)}, u32[]{:S(2)}) async-start(f32[2,64,8,256]{3,1,0,2:T(8,128)} %bitcast.38), calls=%async_computation.1 | async-start | bytes 2097152 | tf_op jit(solution)/shard_map/all_to_all | solution.py:80
  120.2 18.3 %select_multiply_fusion = f32[256,2,512]{2,1,0:T(2,128)S(1)} fusion(pred[256,2]{1,0:T(8,128)(4,1)S(1)} %fusion.34, f32[256,2]{1,0:T(8,128)S(1)} %compare_select_fusion.2, s32[256,2]{1,0:T(8,128)S(1)} %compare_select_fusion.3), kind=kLoop, calls=%fused_computation.40 | loop fusion | flops 4194304 | bytes 1053184 | tf_op jit(solution)/shard_map/mul | solution.py:28
  138.6 0.8 fusion.44
  139.4 0.9 pad_maximum_fusion.1
  140.3 1.8 stack.7
  142.3 4.3 %select_multiply_fusion.1 = f32[8,64,512]{2,1,0:T(8,128)S(1)} fusion(f32[8,64]{1,0:T(8,128)S(1)} %compare_select_fusion.6, s32[8,64]{1,0:T(8,128)S(1)} %compare_select_fusion.7, pred[8,64]{1,0:T(8,128)(4,1)S(1)} %fusion.40), kind=kLoop, calls=%fused_computation.41 | loop fusion | flops 4194304 | bytes 1053184 | tf_op jit(solution)/shard_map/mul | solution.py:28
  146.6 1.4 broadcast_multiply_fusion
  148.0 1.8 fusion.14
  149.9 20.2 %all_to_all.31 = f32[8,64,256]{2,1,0:T(8,128)S(1)} all-to-all(f32[8,64,256]{2,1,0:T(8,128)S(1)} %fusion.14), channel_id=1, replica_groups=mesh['dom'=4,'freq'=8] {'freq'}, dimensions={0} | all-to-all | bytes 1048576 | tf_op jit(solution)/shard_map/all_to_all | solution.py:85
  170.1 0.8 multiply_reduce_fusion
  170.9 0.3 reshape.233
  171.2 0.4 fusion.45
  171.8 4.3 %multiply_reduce_fusion.1 = (f32[]{:T(128)}, f32[32,2,2048]{2,1,0:T(2,128)S(1)}, f32[32,2,2048]{2,1,0:T(2,128)S(1)}) fusion(f32[32,2,2,2048]{3,2,1,0:T(2,128)S(1)} %copy-done.2, f32[32,2048]{1,0:T(8,128)S(1)} %bitcast.51, f32[32,2048]{1,0:T(8,128)S(1)} %bitcast.53), kind=kLoop, calls=%fused_computation.47 | loop fusion | flops 655359 | bytes 2621444 | tf_op jit(solution)/shard_map/reduce_sum | solution.py:91
  176.1 37.6 %all-reduce = (f32[]{:T(128)}, f32[]{:T(128)}) all-reduce(f32[]{:T(128)} %get-tuple-element.65, f32[]{:T(128)} %get-tuple-element.82), channel_id=1, replica_groups=mesh['dom'=4,'freq'=8] {'dom','freq'}, use_global_device_ids=true, to_apply=%region_4.5 | all-reduce | flops 2 | bytes 16 | tf_op jit(solution)/shard_map/psum | solution.py:90
  214.5 0.4 squeeze.23
  214.8 0.4 squeeze.24
  215.2 0.3 mul.219
  215.5 0.4 mul.220
  215.9 0.3 mul.223
  216.1 0.4 mul.224
  217.2 0.9 negate_multiply_fusion
  (45 shorter events, 0.9 us)
Async XLA Ops:
  7.2 106.4 %reduce-scatter.2.cloned.1.call-start = ((), (), s32[]{:S(2)}) async-start(), calls=%async_computation.3 | async-start | bytes 327680 | tf_op jit(solution)/shard_map/reduce_scatter | solution.py:72
  7.2 12.0 %copy-start.4 = (s32[2,4096]{1,0:T(2,128)S(1)}, s32[2,4096]{1,0:T(2,128)}, u32[]{:S(2)}) copy-start(s32[2,4096]{1,0:T(2,128)} %param.10) | copy-start | bytes 98308
  49.9 0.8 copy-start.5
  49.9 0.8 copy-start.6
  51.2 1.3 copy-start.1
  115.6 32.3 %all-to-all-start = ((f32[2,64,8,256]{3,1,0,2:T(8,128)}), f32[2,64,8,256]{3,1,0,2:T(8,128)S(1)}, u32[]{:S(2)}, u32[]{:S(2)}) async-start(f32[2,64,8,256]{3,1,0,2:T(8,128)} %bitcast.38), calls=%async_computation.1 | async-start | bytes 2097152 | tf_op jit(solution)/shard_map/all_to_all | solution.py:80
  148.0 22.1 %copy-start.3 = (f32[64,2048]{1,0:T(8,128)S(1)}, f32[64,2048]{1,0:T(8,128)}, u32[]{:S(2)}) copy-start(f32[64,2048]{1,0:T(8,128)} %param.9) | copy-start | bytes 1572868
  170.1 1.7 copy-start.2
  170.9 5.2 %copy-start = (f32[64,2048]{1,0:T(8,128)}, f32[64,2048]{1,0:T(8,128)S(1)}, u32[]{:S(2)}) copy-start(f32[64,2048]{1,0:T(8,128)S(1)} %get-tuple-element.83) | copy-start | bytes 1572868
Sparse Core Ops, SparseCore 0:
  88.9 24.6 reduce-scatter.1
where the time goes:
time: 227 us; the launch traced here: 226 us
  blocking collectives  68.3 us (30%)
  local copies, waits for them, and re-layouts  38.4 us (17%)
  matrix products  37 us (16%)
  other arithmetic  36.1 us (16%)
  waiting for transfers between devices  24.4 us (11%)
  between operations  17 us (7%)
  starting transfers between devices  4.64 us (2%)
    psum x1, blocking collectives, body(): lax.psum((jnp.sum(raw * raw), jnp.sum(residual * residual)), ('dom', 'fre...  37.6 us
    dot_general x8, matrix products, accumulate(): jnp.dot(flow_piece, signed, precision=lax.Precision.HIGHEST, preferred_el...  35.2 us
    gather x2, local copies, waits for them, and re-layouts, body(): across = extended[:, terminals[0]] - extended[:, terminals[1]]  28.2 us
    reduce_scatter x1, waiting for transfers between devices, body(): lax.psum_scatter(totals[:, :, node_count:], 'dom', scatter_dimension=2, t...  24.4 us
    mul x2, other arithmetic, transform_table(): forward = values * weight[:, None]  22.6 us
    all_to_all x1, blocking collectives, body(): lax.all_to_all(spectra, 'freq', split_axis=0, concat_axis=1, tiled=True)  20.2 us
    all_gather x1, blocking collectives, body(): lax.all_gather(voltages[:, :border_count], 'dom', axis=1, tiled=True)  10.5 us
    all_to_all x1, starting transfers between devices, body(): lax.all_to_all(grouped, 'freq', split_axis=2, concat_axis=1, tiled=True)  4.6 us
  transfers between devices with their start and end apart: 2, of which 1 were waited for; matrix products, arithmetic and copies ran while one was open for 12% of the time, Pallas kernels for 0%

commit v1 on v0

v1 whole, which is shorter than its diff:
```python
import functools
import math

import jax
import jax.numpy as jnp
import numpy as np
from jax import lax
from jax.experimental import pallas as pl
from jax.experimental.pallas import tpu as pltpu
from jax.sharding import PartitionSpec as P

MESH = pl.DeviceIdType.MESH
LANES = 128
VMEM = pltpu.VMEM
trust_radius = 2.0


def fourier_matrix(samples):
    row = np.arange(samples)
    harmonic = row // 2
    sine = row % 2 == 1
    order = np.where(harmonic == 0, np.where(sine, samples // 2, 0), harmonic)
    phase = (order[:, None] * np.arange(samples)[None, :] % samples) * (2.0 * math.pi / samples)
    values = np.where((sine & (harmonic > 0))[:, None], np.sin(phase), np.cos(phase))
    weight = np.where(harmonic == 0, math.sqrt(1.0 / samples), math.sqrt(2.0 / samples))
    full = (values * weight[:, None]).astype(np.float32)
    high = full.astype(jnp.bfloat16)
    low = (full - high.astype(np.float32)).astype(jnp.bfloat16)
    return high, low


def split(x):
    high = x.astype(jnp.bfloat16)
    low = (x - high.astype(jnp.float32)).astype(jnp.bfloat16)
    return high, low


def dot(a, b, contract=((1,), (0,))):
    return lax.dot_general(a, b, (contract, ((), ())), preferred_element_type=jnp.float32)


def flipped(index, mask):
    bit = 1
    while bit <= mask:
        if mask & bit:
            index = index + bit * (1 - 2 * ((index // bit) % 2))
        bit *= 2
    return index


def border_kernel(doms, v_ref, out_ref, send_sem, recv_sem, local_sem):
    me = lax.axis_index("dom")
    barrier = pltpu.get_barrier_semaphore()
    for j in range(1, doms):
        pl.semaphore_signal(barrier, inc=1, device_id={"dom": flipped(me, j)}, device_id_type=MESH)
    pl.semaphore_wait(barrier, doms - 1)
    copies = []
    for j in range(1, doms):
        copy = pltpu.make_async_remote_copy(
            src_ref=v_ref,
            dst_ref=out_ref.at[me],
            send_sem=send_sem.at[j],
            recv_sem=recv_sem.at[me],
            device_id={"dom": flipped(me, j)},
            device_id_type=MESH,
        )
        copy.start()
        copies.append(copy)
    own = pltpu.make_async_copy(v_ref, out_ref.at[me], local_sem)
    own.start()
    own.wait()
    for j in range(1, doms):
        peer = flipped(me, j)
        pltpu.make_async_remote_copy(
            src_ref=v_ref,
            dst_ref=out_ref.at[peer],
            send_sem=send_sem.at[j],
            recv_sem=recv_sem.at[peer],
            device_id={"dom": peer},
            device_id_type=MESH,
        ).wait_recv()
    for copy in copies:
        copy.wait_send()


def circuit_kernel(v_ref, border_ref, term_ref, cur_ref, chg_ref, out_ref, volt, inc, flow):
    rows, nodes = v_ref.shape
    doms, _, border = border_ref.shape
    wide = inc.shape[0]
    elems = inc.shape[1]
    high, low = split(v_ref[...])
    volt[:rows, :nodes] = high
    volt[rows:, :nodes] = low
    for p in range(doms):
        high, low = split(border_ref[p])
        volt[:rows, nodes + p * border : nodes + (p + 1) * border] = high
        volt[rows:, nodes + p * border : nodes + (p + 1) * border] = low
    ew = 512
    kb = 256

    def gather(i, carry):
        cols = pl.ds(pl.multiple_of(i * ew, ew), ew)
        first = term_ref[0:1, cols]
        second = term_ref[1:2, cols]
        total = jnp.zeros((2 * rows, ew), jnp.float32)
        base = lax.broadcasted_iota(jnp.int32, (kb, ew), 0)
        for k in range(wide // kb):
            plus = jnp.where(base == first - k * kb, 1.0, 0.0)
            minus = jnp.where(base == second - k * kb, 1.0, 0.0)
            tile = (plus - minus).astype(jnp.bfloat16)
            inc[k * kb : (k + 1) * kb, cols] = tile
            total = total + dot(volt[:, k * kb : (k + 1) * kb], tile)
        across = total[:rows] + total[rows:]
        current = cur_ref[0:1, cols] * across + cur_ref[1:2, cols] * jnp.tanh(2.0 * across)
        charge = chg_ref[0:1, cols] * across + chg_ref[1:2, cols] * jnp.tanh(across)
        high, low = split(current)
        flow[:rows, cols] = high
        flow[rows : 2 * rows, cols] = low
        high, low = split(charge)
        flow[2 * rows : 3 * rows, cols] = high
        flow[3 * rows :, cols] = low
        return carry

    lax.fori_loop(0, elems // ew, gather, 0)

    def scatter(i, carry):
        mine = pl.ds(pl.multiple_of(i * kb, kb), kb)
        total = dot(flow[...], inc[mine, :], ((1,), (1,)))
        cur = total[:rows] + total[rows : 2 * rows]
        chg = total[2 * rows : 3 * rows] + total[3 * rows :]
        parts = []
        for c in range(kb // LANES):
            parts += [cur[:, c * LANES : (c + 1) * LANES], chg[:, c * LANES : (c + 1) * LANES]]
        out_ref[:, pl.ds(pl.multiple_of(i * 2 * kb, 2 * kb), 2 * kb)] = jnp.concatenate(parts, axis=1)
        return carry

    lax.fori_loop(0, wide // kb, scatter, 0)


def swap_pairs(x):
    even = lax.broadcasted_iota(jnp.int32, x.shape, 0) % 2 == 0
    rows = x.shape[0]
    return jnp.where(even, pltpu.roll(x, rows - 1, 0), pltpu.roll(x, 1, 0))


def newton_kernel(
    doms, freqs, entries,
    t_ref, high_ref, low_ref, src_ref, j0_ref, j1_ref,
    res_ref, step_ref, norm_ref,
    edge, summed, land, spec, back, part_dom, part_freq,
    edge_send, edge_recv, out_send, out_recv, back_send, back_recv,
    pd_send, pd_recv, pf_send, pf_recv, local_sem, local_sem2,
):
    dom = lax.axis_index("dom")
    freq = lax.axis_index("freq")
    rows, nodes = src_ref.shape
    chunks = nodes // freqs // LANES
    pair = 2 * LANES
    samples = rows * freqs
    barrier = pltpu.get_barrier_semaphore()
    for j in range(1, doms):
        pl.semaphore_signal(barrier, inc=1, device_id={"dom": flipped(dom, j)}, device_id_type=MESH)
    for j in range(1, freqs):
        pl.semaphore_signal(barrier, inc=1, device_id={"freq": flipped(freq, j)}, device_id_type=MESH)
    pl.semaphore_wait(barrier, doms + freqs - 2)

    def columns(block):
        return pl.ds(pl.multiple_of(block * pair, pair), pair)

    def edge_copy(j, owner, sender):
        return pltpu.make_async_remote_copy(
            src_ref=t_ref.at[:, columns(nodes // LANES + owner)],
            dst_ref=edge.at[sender],
            send_sem=edge_send.at[j],
            recv_sem=edge_recv.at[sender],
            device_id={"dom": flipped(dom, j)},
            device_id_type=MESH,
        )

    for j in range(1, doms):
        edge_copy(j, flipped(dom, j), dom).start()

    my_rows = pl.ds(pl.multiple_of(freq * rows, rows), rows)

    def out_copy(c, j, source, sender):
        return pltpu.make_async_remote_copy(
            src_ref=source,
            dst_ref=land.at[c, pl.ds(pl.multiple_of(sender * rows, rows), rows), :],
            send_sem=out_send.at[c, j],
            recv_sem=out_recv.at[c, sender],
            device_id={"freq": flipped(freq, j)},
            device_id_type=MESH,
        )

    def block_of(c, peer):
        return t_ref.at[:, columns(peer * chunks + c)]

    for c in range(chunks):
        for j in range(freqs - 1, 0, -1):
            peer = flipped(freq, j)
            if c == 0:
                @pl.when(peer != 0)
                def _():
                    out_copy(c, j, block_of(c, peer), freq).start()
            else:
                out_copy(c, j, block_of(c, peer), freq).start()

    for j in range(1, doms):
        edge_copy(j, dom, flipped(dom, j)).wait_recv()
    total = t_ref[:, :pair] + t_ref[:, columns(nodes // LANES + dom)]
    for p in range(doms):
        total = total + jnp.where(dom == p, 0.0, edge[p])
    summed[...] = total
    for j in range(freqs - 1, 0, -1):
        @pl.when(flipped(freq, j) == 0)
        def _():
            out_copy(0, j, summed, freq).start()

    for c in range(chunks):
        if c == 0:
            @pl.when(freq == 0)
            def _():
                land[0, my_rows, :] = total

            @pl.when(freq != 0)
            def _():
                land[0, my_rows, :] = t_ref[:, columns(freq * chunks)]
        else:
            land[c, my_rows, :] = t_ref[:, columns(freq * chunks + c)]

    def back_copy(c, j, target, sender):
        return pltpu.make_async_remote_copy(
            src_ref=spec.at[c, pl.ds(pl.multiple_of(target * rows, rows), rows), :],
            dst_ref=back.at[:, pl.ds(pl.multiple_of((sender * chunks + c) * LANES, LANES), LANES)],
            send_sem=back_send.at[c, j],
            recv_sem=back_recv.at[c, sender],
            device_id={"freq": flipped(freq, j)},
            device_id_type=MESH,
        )

    row = lax.broadcasted_iota(jnp.int32, (samples, LANES), 0)
    rate = (row // 2).astype(jnp.float32) * (2.0 / samples)
    rate = jnp.where(row % 2 == 0, rate, -rate)
    for c in range(chunks):
        for j in range(freqs - 1, 0, -1):
            peer = flipped(freq, j)
            out_copy(c, j, summed, peer).wait_recv()
        high, low = split(land[c])
        product = dot(high_ref[...], high) + (dot(high_ref[...], low) + dot(low_ref[...], high))
        spec[c] = product[:, :LANES] + rate * swap_pairs(product[:, LANES:])
        for j in range(freqs - 1, 0, -1):
            back_copy(c, j, flipped(freq, j), freq).start()
        back[:, pl.ds(pl.multiple_of((freq * chunks + c) * LANES, LANES), LANES)] = spec[c, my_rows, :]

    for c in range(chunks):
        for j in range(freqs - 1, 0, -1):
            peer = flipped(freq, j)
            back_copy(c, j, peer, peer).wait_recv()

    width = 2 * LANES
    raw_total = jnp.zeros((1, width), jnp.float32)
    res_total = jnp.zeros((1, width), jnp.float32)
    even = lax.broadcasted_iota(jnp.int32, (rows, width), 0) % 2 == 0
    for b in range(nodes // width):
        cols = slice(b * width, (b + 1) * width)
        residual = back[:, cols] - src_ref[:, cols]
        res_ref[:, cols] = residual
        upper = jnp.where(even, residual, pltpu.roll(residual, 1, 0))
        lower = jnp.where(even, pltpu.roll(residual, rows - 1, 0), residual)
        raw = -(j0_ref[:, cols] * upper + j1_ref[:, cols] * lower)
        step_ref[:, cols] = raw
        raw_total = raw_total + jnp.sum(raw * raw, axis=0, keepdims=True)
        res_total = res_total + jnp.sum(residual * residual, axis=0, keepdims=True)
    raw_sum = jnp.sum(raw_total, axis=1, keepdims=True)
    res_sum = jnp.sum(res_total, axis=1, keepdims=True)
    lane = lax.broadcasted_iota(jnp.int32, (8, LANES), 1)
    part_dom[dom] = jnp.where(lane == 0, raw_sum, jnp.where(lane == 1, res_sum, 0.0))

    def reduce_over(axis, count, me, part, send, recv):
        def copy_of(j, sender):
            return pltpu.make_async_remote_copy(
                src_ref=part.at[me],
                dst_ref=part.at[sender],
                send_sem=send.at[j],
                recv_sem=recv.at[sender],
                device_id={axis: flipped(me, j)},
                device_id_type=MESH,
            )

        for j in range(count - 1, 0, -1):
            copy_of(j, me).start()
        for j in range(count - 1, 0, -1):
            copy_of(j, flipped(me, j)).wait_recv()
        return sum((part[i] for i in range(1, count)), part[0])

    part_freq[freq] = reduce_over("dom", doms, dom, part_dom, pd_send, pd_recv)
    both = reduce_over("freq", freqs, freq, part_freq, pf_send, pf_recv)
    raw_sum = jnp.sum(jnp.where(lane == 0, both, 0.0)[:1], axis=1, keepdims=True)
    res_sum = jnp.sum(jnp.where(lane == 1, both, 0.0)[:1], axis=1, keepdims=True)
    spread = jnp.sqrt(raw_sum / entries + 1e-06)
    scale = jnp.minimum(1.0, trust_radius / spread)
    norm_ref[...] = jnp.broadcast_to(jnp.sqrt(res_sum), (8, LANES))
    for b in range(nodes // width):
        cols = slice(b * width, (b + 1) * width)
        step_ref[:, cols] = step_ref[:, cols] * scale

    for j in range(1, doms):
        edge_copy(j, flipped(dom, j), dom).wait_send()
    for c in range(chunks):
        for j in range(1, freqs):
            out_copy(c, j, summed, freq).wait_send()
            back_copy(c, j, flipped(freq, j), freq).wait_send()
    for axis, count, me, part, send, recv in (
        ("dom", doms, dom, part_dom, pd_send, pd_recv),
        ("freq", freqs, freq, part_freq, pf_send, pf_recv),
    ):
        for j in range(1, count):
            pltpu.make_async_remote_copy(
                src_ref=part.at[me],
                dst_ref=part.at[me],
                send_sem=send.at[j],
                recv_sem=recv.at[me],
                device_id={axis: flipped(me, j)},
                device_id_type=MESH,
            ).wait_send()


def body(doms, freqs, voltages, sources, terminals, elem_current, elem_charge, jacobi):
    rows, nodes = voltages.shape
    elems = terminals.shape[1]
    border = nodes // 16
    wide = nodes + doms * border
    samples = rows * freqs
    chunks = nodes // freqs // LANES
    f32, bf16 = jnp.float32, jnp.bfloat16
    dma = pltpu.SemaphoreType.DMA
    limit = 60 * 1024 * 1024
    vmem = pl.BlockSpec(memory_space=VMEM)
    edges = pl.pallas_call(
        functools.partial(border_kernel, doms),
        grid=(1,),
        out_shape=jax.ShapeDtypeStruct((doms, rows, border), f32),
        in_specs=[pl.BlockSpec((rows, border), lambda i: (0, 0))],
        out_specs=vmem,
        scratch_shapes=[dma((doms,)), dma((doms,)), dma(())],
        compiler_params=pltpu.CompilerParams(collective_id=0, has_side_effects=True),
    )(voltages)
    totals = pl.pallas_call(
        circuit_kernel,
        out_shape=jax.ShapeDtypeStruct((rows, 2 * wide), f32),
        in_specs=[vmem] * 5,
        out_specs=vmem,
        scratch_shapes=[
            VMEM((2 * rows, wide), bf16),
            VMEM((wide, elems), bf16),
            VMEM((4 * rows, elems), bf16),
        ],
        compiler_params=pltpu.CompilerParams(vmem_limit_bytes=limit),
    )(voltages, edges, terminals, elem_current, elem_charge)
    high, low = fourier_matrix(samples)
    residual, step, norm = pl.pallas_call(
        functools.partial(newton_kernel, doms, freqs, float(samples * nodes * doms)),
        out_shape=(
            jax.ShapeDtypeStruct((rows, nodes), f32),
            jax.ShapeDtypeStruct((rows, nodes), f32),
            jax.ShapeDtypeStruct((8, LANES), f32),
        ),
        in_specs=[vmem] * 6,
        out_specs=(vmem,) * 3,
        scratch_shapes=[
            VMEM((doms, rows, 2 * LANES), f32),
            VMEM((rows, 2 * LANES), f32),
            VMEM((chunks, samples, 2 * LANES), f32),
            VMEM((chunks, samples, LANES), f32),
            VMEM((rows, nodes), f32),
            VMEM((doms, 8, LANES), f32),
            VMEM((freqs, 8, LANES), f32),
            dma((doms,)), dma((doms,)),
            dma((chunks, freqs)), dma((chunks, freqs)),
            dma((chunks, freqs)), dma((chunks, freqs)),
            dma((doms,)), dma((doms,)),
            dma((freqs,)), dma((freqs,)),
            dma(()), dma(()),
        ],
        compiler_params=pltpu.CompilerParams(
            collective_id=1, has_side_effects=True, vmem_limit_bytes=limit
        ),
    )(
        totals, jnp.asarray(high), jnp.asarray(low), sources,
        jacobi[:, :, 0, :].reshape(rows, nodes), jacobi[:, :, 1, :].reshape(rows, nodes),
    )
    return residual, step, norm[0, 0]


def solution(mesh):
    placed = (
        P("freq", "dom"),
        P("freq", "dom"),
        P(None, "dom"),
        P(None, "dom"),
        P(None, "dom"),
        P("freq", None, None, "dom"),
    )
    return jax.shard_map(
        functools.partial(body, mesh.shape["dom"], mesh.shape["freq"]),
        mesh=mesh,
        in_specs=placed,
        out_specs=(P("freq", "dom"), P("freq", "dom"), P()),
        check_vma=False,
    )
```

time: 227 us -> 93.1 us (0.41)
  Pallas kernels: 0 us -> 80.7 us
  blocking collectives: 68.3 us -> 0 us
  matrix products: 37 us -> 0 us
  other arithmetic: 36.1 us -> 0 us
  local copies, waits for them, and re-layouts: 38.4 us -> 11.4 us
  waiting for transfers between devices: 24.4 us -> 0 us
  between operations: 17 us -> 0.66 us
  starting transfers between devices: 4.64 us -> 0 us
    pallas_call x0 -> x3, Pallas kernels: none -> 80.7 us  [the longest x1 51.3 us: body(): pl.pallas_call(functools.partial(newton_kernel, doms, freqs, float(sample...]
    psum x1 -> x0, blocking collectives: 37.6 us -> none  [body(): lax.psum((jnp.sum(raw * raw), jnp.sum(residual * residual)), ('dom', 'fre...]
    dot_general x9 -> x0, matrix products: 37 us -> none  [the longest x8 35.2 us: accumulate(): jnp.dot(flow_piece, signed, precision=lax.Precision.HIGHEST, preferred_el...]
    gather x2 -> x0, local copies, waits for them, and re-layouts: 28.2 us -> none  [body(): across = extended[:, terminals[0]] - extended[:, terminals[1]]]
    mul x5 -> x0, other arithmetic: 24.9 us -> none  [the longest x2 22.6 us: transform_table(): forward = values * weight[:, None]]
    reduce_scatter x1 -> x0, waiting for transfers between devices: 24.4 us -> none  [body(): lax.psum_scatter(totals[:, :, node_count:], 'dom', scatter_dimension=2, t...]
    all_to_all x1 -> x0, blocking collectives: 20.2 us -> none  [body(): lax.all_to_all(spectra, 'freq', split_axis=0, concat_axis=1, tiled=True)]
    all_gather x1 -> x0, blocking collectives: 10.5 us -> none  [body(): lax.all_gather(voltages[:, :border_count], 'dom', axis=1, tiled=True)]
  transfers between devices with their start and end apart: 2 -> 0, of which waited for: 1 -> 0; matrix products, arithmetic and copies ran while one was open for 12% -> 0% of each run, Pallas kernels for 0% -> 0%
where the time goes in v1:
time: 93.1 us; the launch traced here: 92.7 us
  Pallas kernels  80.7 us (87%)
  local copies, waits for them, and re-layouts  11.4 us (12%)
    pallas_call x1, Pallas kernels, body(): pl.pallas_call(functools.partial(newton_kernel, doms, freqs, float(sample...  51.3 us
    pallas_call x1, Pallas kernels, body(): pl.pallas_call(circuit_kernel, out_shape=jax.ShapeDtypeStruct((rows, 2 *...  21.2 us
    pallas_call x1, Pallas kernels, body(): pl.pallas_call(functools.partial(border_kernel, doms), grid=(1,), out_sha...  8.23 us
    slice x1, local copies, waits for them, and re-layouts, body(): jacobi[:, :, 1, :].reshape(rows, nodes)  5.13 us
    unnamed x4, local copies, waits for them, and re-layouts  2.67 us

profile of v1, /device:TPU:0, one launch (start us, length us, event | category | flops | bytes accessed | tf_op | source)
XLA Modules:
  0.0 92.7 jit_solution(16219669792425032762)
XLA Ops:
  0.6 8.2 %shard_map.103.border_ref = f32[4,64,128]{2,1,0:T(8,128)} custom-call(f32[64,2048]{1,0:T(8,128)} %v_ref.3), custom_call_target="tpu_custom_call" | custom-call | tf_op jit(solution)/shard_map/pallas_call | solution.py:339
  8.9 5.1 %slice_reduce_fusion = (f32[32,2,2048]{2,1,0:T(2,128)S(1)}, f32[32,2,2048]{2,1,0:T(2,128)S(1)}) fusion(f32[32,2,2,2048]{3,2,1,0:T(2,128)} %param.13), kind=kLoop, calls=%fused_computation | loop fusion | bytes 2097152 | tf_op jit(solution)/shard_map/slice | solution.py:390
  14.0 1.2 %reshape_squeeze.7.j1_ref = f32[64,2048]{1,0:T(8,128)} reshape(f32[32,2,2048]{2,1,0:T(2,128)S(1)} %get-tuple-element.9) | data formatting | bytes 1048576 | tf_op jit(solution)/shard_map/reshape;squeeze | solution.py:390
  15.2 1.2 %reshape_squeeze.6.j0_ref = f32[64,2048]{1,0:T(8,128)} reshape(f32[32,2,2048]{2,1,0:T(2,128)S(1)} %get-tuple-element.10) | data formatting | bytes 1048576 | tf_op jit(solution)/shard_map/reshape;squeeze | solution.py:390
  16.3 21.2 %shard_map.104.t_ref = f32[64,5120]{1,0:T(8,128)} custom-call(f32[64,2048]{1,0:T(8,128)} %v_ref.3, f32[4,64,128]{2,1,0:T(8,128)} %shard_map.103.border_ref, s32[2,4096]{1,0:T(2,128)} %term_ref.1, f32[2,4096]{1,0:T(2,128)} %cur_ref.1, f32[2,4096]{1,0:T(2,128)} %chg_ref.1), custom_call_target="tpu_custom_call" | custom-call | tf_op jit(solution)/shard_map/pallas_call | solution.py:348
  37.5 51.3 %shard_map.105 = (f32[64,2048]{1,0:T(8,128)}, f32[64,2048]{1,0:T(8,128)}, f32[8,128]{1,0:T(8,128)}) custom-call(f32[64,5120]{1,0:T(8,128)} %shard_map.104.t_ref, bf16[512,512]{1,0:T(8,128)(2,1)} %constant.4.clone.high_ref, bf16[512,512]{1,0:T(8,128)(2,1)} %constant.5.clone.low_ref, f32[64,2048]{1,0:T(8,128)} %src_ref.1, f32[64,2048]{1,0:T(8,128)} %reshape_squeeze.6.j0_ref, ...), custom_call_target="tpu_custom_call" | custom-call | tf_op jit(solution)/shard_map/pallas_call | solution.py:361
  88.8 0.0 copy-start
  88.8 1.3 %slice.11 = f32[1,1]{1,0:T(1,128)} slice(f32[8,128]{1,0:T(8,128)} %get-tuple-element.8), slice={[0:1], [0:1]} | slice | bytes 8 | tf_op jit(solution)/shard_map/slice | solution.py:392
  90.1 1.9 %copy.15 = f32[64,2048]{1,0:T(8,128)} copy(f32[64,2048]{1,0:T(8,128)} %get-tuple-element.14) | data formatting | bytes 1048576
  91.9 0.0 copy-done
  92.0 0.8 copy.16
Async XLA Ops:
  88.8 3.1 %copy-start = (f32[64,2048]{1,0:T(8,128)S(1)}, f32[64,2048]{1,0:T(8,128)}, u32[]{:S(2)}) copy-start(f32[64,2048]{1,0:T(8,128)} %get-tuple-element.15) | copy-start | bytes 1572868

commit v2 on v0

v2 whole, which is shorter than its diff:
```python
import functools
import math

import jax
import jax.numpy as jnp
import numpy as np
from jax import lax
from jax.experimental import pallas as pl
from jax.experimental.pallas import tpu as pltpu
from jax.sharding import PartitionSpec as P

MESH = pl.DeviceIdType.MESH
LANES = 128
VMEM = pltpu.VMEM
trust_radius = 2.0


def fourier_matrix(samples):
    row = np.arange(samples)
    harmonic = row // 2
    sine = row % 2 == 1
    order = np.where(harmonic == 0, np.where(sine, samples // 2, 0), harmonic)
    phase = (order[:, None] * np.arange(samples)[None, :] % samples) * (2.0 * math.pi / samples)
    values = np.where((sine & (harmonic > 0))[:, None], np.sin(phase), np.cos(phase))
    weight = np.where(harmonic == 0, math.sqrt(1.0 / samples), math.sqrt(2.0 / samples))
    full = (values * weight[:, None]).astype(np.float32)
    high = full.astype(jnp.bfloat16)
    low = (full - high.astype(np.float32)).astype(jnp.bfloat16)
    return high, low


def split(x):
    high = x.astype(jnp.bfloat16)
    low = (x - high.astype(jnp.float32)).astype(jnp.bfloat16)
    return high, low


def dot(a, b, contract=((1,), (0,))):
    return lax.dot_general(a, b, (contract, ((), ())), preferred_element_type=jnp.float32)


def xor(a, b, count):
    out, bit = 0, 1
    while bit < count:
        out = out + bit * ((a // bit + b // bit) % 2)
        bit *= 2
    return out


def swap_pairs(x):
    even = lax.broadcasted_iota(jnp.int32, x.shape, 0) % 2 == 0
    rows = x.shape[0]
    return jnp.where(even, pltpu.roll(x, rows - 1, 0), pltpu.roll(x, 1, 0))


def kernel(
    doms, freqs, entries,
    v_ref, term_ref, cur_ref, chg_ref, high_any, low_any, src_any, jac_any,
    back, raw_ref, norm_ref, scale_ref,
    volt, seen, inc, partial, flow, stage, edge_out, edge, land, spec, high_ref, low_ref, src_ref,
    jac_ref, part_dom, part_freq,
    v_send, v_recv, edge_send, edge_recv, out_send, out_recv, back_send, back_recv,
    pd_send, pd_recv, pf_send, pf_recv, load_sem,
):
    dom = lax.axis_index("dom")
    freq = lax.axis_index("freq")
    rows, nodes = v_ref.shape
    wide, elems = inc.shape
    border = seen.shape[2]
    samples = rows * freqs
    block = nodes // freqs
    chunks = block // LANES
    pair = 2 * LANES
    ew = 512
    kb = 256

    barrier = pltpu.get_barrier_semaphore()
    for j in range(1, doms):
        pl.semaphore_signal(barrier, inc=1, device_id={"dom": xor(dom, j, doms)}, device_id_type=MESH)
    for j in range(1, freqs):
        pl.semaphore_signal(barrier, inc=1, device_id={"freq": xor(freq, j, freqs)}, device_id_type=MESH)

    loads = [
        pltpu.make_async_copy(a, b, load_sem.at[i])
        for i, (a, b) in enumerate(
            ((high_any, high_ref), (low_any, low_ref), (src_any, src_ref), (jac_any, jac_ref))
        )
    ]
    for load in loads:
        load.start()

    def dom_copy(j, source, target, send, recv, sender):
        return pltpu.make_async_remote_copy(
            src_ref=source,
            dst_ref=target.at[sender],
            send_sem=send.at[j],
            recv_sem=recv.at[sender],
            device_id={"dom": xor(dom, j, doms)},
            device_id_type=MESH,
        )

    def v_copy(j, sender):
        return dom_copy(j, v_ref.at[:, :border], seen, v_send, v_recv, sender)

    def edge_copy(j, owner, sender):
        return dom_copy(j, edge_out.at[owner], edge, edge_send, edge_recv, sender)

    high, low = split(v_ref[...])
    volt[:rows, :nodes] = high
    volt[rows:, :nodes] = low

    def build(i, carry):
        @pl.when(i == 1)
        def _():
            pl.semaphore_wait(barrier, doms + freqs - 2)
            for j in range(doms - 1, 0, -1):
                v_copy(j, dom).start()

        cols = pl.ds(pl.multiple_of(i * ew, ew), ew)
        first = term_ref[0:1, cols]
        second = term_ref[1:2, cols]
        same = first == second
        first = jnp.where(same, -1, first)
        second = jnp.where(same, -1, second)
        total = jnp.zeros((2 * rows, ew), jnp.float32)
        base = lax.broadcasted_iota(jnp.int32, (kb, ew), 0)
        for k in range(wide // kb):
            tile = jnp.where(base == first - k * kb, 1.0, jnp.where(base == second - k * kb, -1.0, 0.0))
            tile = tile.astype(jnp.bfloat16)
            inc[k * kb : (k + 1) * kb, cols] = tile
            if k * kb < nodes:
                total = total + dot(volt[:, k * kb : (k + 1) * kb], tile)
        partial[:, cols] = total[:rows] + total[rows:]
        return carry

    lax.fori_loop(0, elems // ew, build, 0)

    seen[dom] = v_ref[:, :border]
    for j in range(1, doms):
        v_copy(j, xor(dom, j, doms)).wait_recv()
    for p in range(doms):
        high, low = split(seen[p])
        volt[:rows, nodes + p * border : nodes + (p + 1) * border] = high
        volt[rows:, nodes + p * border : nodes + (p + 1) * border] = low

    def evaluate(i, carry):
        cols = pl.ds(pl.multiple_of(i * ew, ew), ew)
        total = dot(volt[:, nodes:], inc[nodes:, cols])
        across = partial[:, cols] + (total[:rows] + total[rows:])
        current = cur_ref[0:1, cols] * across + cur_ref[1:2, cols] * jnp.tanh(2.0 * across)
        charge = chg_ref[0:1, cols] * across + chg_ref[1:2, cols] * jnp.tanh(across)
        high, low = split(current)
        flow[:rows, cols] = high
        flow[rows : 2 * rows, cols] = low
        high, low = split(charge)
        flow[2 * rows : 3 * rows, cols] = high
        flow[3 * rows :, cols] = low
        return carry

    lax.fori_loop(0, elems // ew, evaluate, 0)

    def scatter(start, width):
        total = dot(flow[...], inc[pl.ds(pl.multiple_of(start, LANES), width), :], ((1,), (1,)))
        cur = total[:rows] + total[rows : 2 * rows]
        chg = total[2 * rows : 3 * rows] + total[3 * rows :]
        return [
            jnp.concatenate([cur[:, c * LANES : (c + 1) * LANES], chg[:, c * LANES : (c + 1) * LANES]], axis=1)
            for c in range(width // LANES)
        ]

    per = kb // LANES

    def border_block(i, carry):
        pieces = scatter(nodes + i * kb, kb)
        for c in range(per):
            edge_out[i * per + c] = pieces[c]
        return carry

    lax.fori_loop(0, (wide - nodes) // kb, border_block, 0)
    for j in range(doms - 1, 0, -1):
        edge_copy(j, xor(dom, j, doms), dom).start()

    my_rows = pl.ds(pl.multiple_of(freq * rows, rows), rows)

    def out_copy(c, j, sender):
        peer = xor(freq, j, freqs)
        return pltpu.make_async_remote_copy(
            src_ref=stage.at[c, peer],
            dst_ref=land.at[c, pl.ds(pl.multiple_of(sender * rows, rows), rows), :],
            send_sem=out_send.at[c, j],
            recv_sem=out_recv.at[c, sender],
            device_id={"freq": peer},
            device_id_type=MESH,
        )

    def node_block(i, carry):
        j = freqs - 1 - i
        peer = xor(freq, j, freqs)
        pieces = scatter(peer * block, block)
        for c in range(chunks):
            stage[c, peer] = pieces[c]

        @pl.when(peer == 0)
        def _():
            for k in range(1, doms):
                edge_copy(k, dom, xor(dom, k, doms)).wait_recv()
            total = stage[0, 0] + edge_out[dom]
            for p in range(doms):
                total = total + jnp.where(dom == p, 0.0, edge[p])
            stage[0, 0] = total

        @pl.when(j != 0)
        def _():
            out_copy(0, j, freq).start()

        return carry

    lax.fori_loop(0, freqs, node_block, 0)

    def later(i, carry):
        for c in range(1, chunks):
            out_copy(c, freqs - 1 - i, freq).start()
        return carry

    if chunks > 1:
        lax.fori_loop(0, freqs - 1, later, 0)

    for c in range(chunks):
        land[c, my_rows, :] = stage[c, freq]

    def back_columns(c, sender):
        return pl.ds(pl.multiple_of((sender * chunks + c) * LANES, LANES), LANES)

    def back_copy(c, j, target, sender):
        return pltpu.make_async_remote_copy(
            src_ref=spec.at[c, pl.ds(pl.multiple_of(target * rows, rows), rows), :],
            dst_ref=back.at[:, back_columns(c, sender)],
            send_sem=back_send.at[c, j],
            recv_sem=back_recv.at[c, sender],
            device_id={"freq": xor(freq, j, freqs)},
            device_id_type=MESH,
        )

    for load in loads:
        load.wait()
    row = lax.broadcasted_iota(jnp.int32, (samples, LANES), 0)
    rate = (row // 2).astype(jnp.float32) * (2.0 / samples)
    rate = jnp.where(row % 2 == 0, rate, -rate)
    for c in range(chunks):
        def arrived(i, carry):
            out_copy(c, freqs - 1 - i, xor(freq, freqs - 1 - i, freqs)).wait_recv()
            return carry

        lax.fori_loop(0, freqs - 1, arrived, 0)
        high, low = split(land[c])
        product = dot(high_ref[...], high) + (dot(high_ref[...], low) + dot(low_ref[...], high))
        spec[c] = product[:, :LANES] + rate * swap_pairs(product[:, LANES:])

        def give(i, carry):
            j = freqs - 1 - i
            back_copy(c, j, xor(freq, j, freqs), freq).start()
            return carry

        lax.fori_loop(0, freqs - 1, give, 0)
        back[:, back_columns(c, freq)] = spec[c, my_rows, :]

    even = lax.broadcasted_iota(jnp.int32, (rows, LANES), 0) % 2 == 0
    sums = (jnp.zeros((8, LANES), jnp.float32), jnp.zeros((8, LANES), jnp.float32))

    def fold(x):
        return jnp.sum((x * x).reshape(rows // 8, 8, LANES), axis=0)

    for c in range(chunks):
        def finish(j, carry):
            peer = xor(freq, j, freqs)

            @pl.when(j != 0)
            def _():
                back_copy(c, j, peer, peer).wait_recv()

            cols = back_columns(c, peer)
            residual = back[:, cols] - src_ref[:, cols]
            upper = jnp.where(even, residual, pltpu.roll(residual, 1, 0))
            lower = jnp.where(even, pltpu.roll(residual, rows - 1, 0), residual)
            raw = -(jac_ref[:, 0, cols] * upper + jac_ref[:, 1, cols] * lower)
            raw_ref[:, cols] = raw
            return carry[0] + fold(raw), carry[1] + fold(residual)

        sums = lax.fori_loop(0, freqs, finish, sums)

    def whole(x):
        return jnp.sum(jnp.sum(x, axis=0, keepdims=True), axis=1, keepdims=True)

    lane = lax.broadcasted_iota(jnp.int32, (8, LANES), 1)
    part_dom[dom] = jnp.where(lane == 0, whole(sums[0]), jnp.where(lane == 1, whole(sums[1]), 0.0))

    def part_copy(axis, count, me, part, send, recv, j, sender):
        return pltpu.make_async_remote_copy(
            src_ref=part.at[me],
            dst_ref=part.at[sender],
            send_sem=send.at[j],
            recv_sem=recv.at[sender],
            device_id={axis: xor(me, j, count)},
            device_id_type=MESH,
        )

    def reduce_over(axis, count, me, part, send, recv):
        for j in range(count - 1, 0, -1):
            part_copy(axis, count, me, part, send, recv, j, me).start()
        for j in range(count - 1, 0, -1):
            part_copy(axis, count, me, part, send, recv, j, xor(me, j, count)).wait_recv()
        return sum((part[i] for i in range(1, count)), part[0])

    part_freq[freq] = reduce_over("dom", doms, dom, part_dom, pd_send, pd_recv)
    both = reduce_over("freq", freqs, freq, part_freq, pf_send, pf_recv)
    raw_sum = jnp.sum(jnp.where(lane == 0, both, 0.0)[:1], axis=1, keepdims=True)
    res_sum = jnp.sum(jnp.where(lane == 1, both, 0.0)[:1], axis=1, keepdims=True)
    spread = jnp.sqrt(raw_sum / entries + 1e-06)
    scale_ref[...] = jnp.minimum(1.0, trust_radius / spread)
    norm_ref[...] = jnp.sqrt(res_sum)

    for j in range(1, doms):
        v_copy(j, dom).wait_send()
        edge_copy(j, dom, dom).wait_send()
        part_copy("dom", doms, dom, part_dom, pd_send, pd_recv, j, dom).wait_send()

    def drain(i, carry):
        j = i + 1
        for c in range(chunks):
            out_copy(c, j, freq).wait_send()
            back_copy(c, j, freq, freq).wait_send()
        part_copy("freq", freqs, freq, part_freq, pf_send, pf_recv, j, freq).wait_send()
        return carry

    lax.fori_loop(0, freqs - 1, drain, 0)


def body(doms, freqs, voltages, sources, terminals, elem_current, elem_charge, jacobi):
    rows, nodes = voltages.shape
    elems = terminals.shape[1]
    border = nodes // 16
    wide = nodes + doms * border
    samples = rows * freqs
    chunks = nodes // freqs // LANES
    f32, bf16 = jnp.float32, jnp.bfloat16
    dma = pltpu.SemaphoreType.DMA
    vmem = pl.BlockSpec(memory_space=VMEM)
    anywhere = pl.BlockSpec(memory_space=pl.ANY)
    high, low = fourier_matrix(samples)
    back, raw, norm, scale = pl.pallas_call(
        functools.partial(kernel, doms, freqs, float(samples * nodes * doms)),
        out_shape=(
            jax.ShapeDtypeStruct((rows, nodes), f32),
            jax.ShapeDtypeStruct((rows, nodes), f32),
            jax.ShapeDtypeStruct((1, 1), f32),
            jax.ShapeDtypeStruct((1, 1), f32),
        ),
        in_specs=[vmem] * 4 + [anywhere] * 4,
        out_specs=(vmem,) * 4,
        scratch_shapes=[
            VMEM((2 * rows, wide), bf16),
            VMEM((doms, rows, border), f32),
            VMEM((wide, elems), bf16),
            VMEM((rows, elems), f32),
            VMEM((4 * rows, elems), bf16),
            VMEM((chunks, freqs, rows, 2 * LANES), f32),
            VMEM((doms, rows, 2 * LANES), f32),
            VMEM((doms, rows, 2 * LANES), f32),
            VMEM((chunks, samples, 2 * LANES), f32),
            VMEM((chunks, samples, LANES), f32),
            VMEM((samples, samples), bf16),
            VMEM((samples, samples), bf16),
            VMEM((rows, nodes), f32),
            VMEM((rows, 2, nodes), f32),
            VMEM((doms, 8, LANES), f32),
            VMEM((freqs, 8, LANES), f32),
            dma((doms,)), dma((doms,)),
            dma((doms,)), dma((doms,)),
            dma((chunks, freqs)), dma((chunks, freqs)),
            dma((chunks, freqs)), dma((chunks, freqs)),
            dma((doms,)), dma((doms,)),
            dma((freqs,)), dma((freqs,)),
            dma((4,)),
        ],
        compiler_params=pltpu.CompilerParams(
            collective_id=0, has_side_effects=True, vmem_limit_bytes=60 * 1024 * 1024
        ),
    )(
        voltages, terminals, elem_current, elem_charge,
        jnp.asarray(high), jnp.asarray(low), sources, jacobi.reshape(rows, 2, nodes),
    )
    return back - sources, raw * scale, norm.reshape(())


def solution(mesh):
    placed = (
        P("freq", "dom"),
        P("freq", "dom"),
        P(None, "dom"),
        P(None, "dom"),
        P(None, "dom"),
        P("freq", None, None, "dom"),
    )
    return jax.shard_map(
        functools.partial(body, mesh.shape["dom"], mesh.shape["freq"]),
        mesh=mesh,
        in_specs=placed,
        out_specs=(P("freq", "dom"), P("freq", "dom"), P()),
        check_vma=False,
    )
```

time: 227 us -> 74.2 us (0.33)
  Pallas kernels: 0 us -> 68.3 us
  blocking collectives: 68.3 us -> 0 us
  local copies, waits for them, and re-layouts: 38.4 us -> 0.01 us
  matrix products: 37 us -> 0 us
  other arithmetic: 36.1 us -> 3.35 us
  waiting for transfers between devices: 24.4 us -> 0 us
  between operations: 17 us -> 2.43 us
  starting transfers between devices: 4.64 us -> 0 us
    pallas_call x0 -> x1, Pallas kernels: none -> 68.3 us  [body(): pl.pallas_call(functools.partial(kernel, doms, freqs, float(samples * nod...]
    psum x1 -> x0, blocking collectives: 37.6 us -> none  [body(): lax.psum((jnp.sum(raw * raw), jnp.sum(residual * residual)), ('dom', 'fre...]
    dot_general x9 -> x0, matrix products: 37 us -> none  [the longest x8 35.2 us: accumulate(): jnp.dot(flow_piece, signed, precision=lax.Precision.HIGHEST, preferred_el...]
    gather x2 -> x0, local copies, waits for them, and re-layouts: 28.2 us -> none  [body(): across = extended[:, terminals[0]] - extended[:, terminals[1]]]
    reduce_scatter x1 -> x0, waiting for transfers between devices: 24.4 us -> none  [body(): lax.psum_scatter(totals[:, :, node_count:], 'dom', scatter_dimension=2, t...]
    mul x5 -> x1, other arithmetic: 24.9 us -> 1.4 us  [body(): return (back - sources, raw * scale, norm.reshape(()))]
    all_to_all x1 -> x0, blocking collectives: 20.2 us -> none  [body(): lax.all_to_all(spectra, 'freq', split_axis=0, concat_axis=1, tiled=True)]
    all_gather x1 -> x0, blocking collectives: 10.5 us -> none  [body(): lax.all_gather(voltages[:, :border_count], 'dom', axis=1, tiled=True)]
  transfers between devices with their start and end apart: 2 -> 0, of which waited for: 1 -> 0; matrix products, arithmetic and copies ran while one was open for 12% -> 0% of each run, Pallas kernels for 0% -> 0%
where the time goes in v2:
time: 74.2 us; the launch traced here: 74 us
  Pallas kernels  68.3 us (92%)
  other arithmetic  3.35 us (5%)
  between operations  2.43 us (3%)
    pallas_call x1, Pallas kernels, body(): pl.pallas_call(functools.partial(kernel, doms, freqs, float(samples * nod...  68.3 us
    sub x1, other arithmetic, body(): return (back - sources, raw * scale, norm.reshape(()))  1.95 us

profile of v2, /device:TPU:0, one launch (start us, length us, event | category | flops | bytes accessed | tf_op | source)
XLA Modules:
  0.0 74.0 jit_solution(16810804843870422617)
XLA Ops:
  0.6 0.0 copy-start
  0.6 68.3 %shard_map.103 = (f32[64,2048]{1,0:T(8,128)}, f32[64,2048]{1,0:T(8,128)}, f32[1,1]{1,0:T(1,128)}, f32[1,1]{1,0:T(1,128)}) custom-call(f32[64,2048]{1,0:T(8,128)} %v_ref.1, s32[2,4096]{1,0:T(2,128)} %term_ref.1, f32[2,4096]{1,0:T(2,128)} %cur_ref.1, f32[2,4096]{1,0:T(2,128)} %chg_ref.1, bf16[512,512]{1,0:T(8,128)(2,1)} %constant.4.clone.high_any, ...), custom_call_target="tpu_custom_call" | custom-call | tf_op jit(solution)/shard_map/pallas_call | solution.py:350
  68.9 0.0 copy-done
  68.9 0.0 copy-start.1
  68.9 1.9 %sub.3 = f32[64,2048]{1,0:T(8,128)} subtract(f32[64,2048]{1,0:T(8,128)} %get-tuple-element.7, f32[64,2048]{1,0:T(8,128)S(1)} %copy-done) | non-fusion elementwise | flops 131072 | bytes 1572864 | tf_op jit(solution)/shard_map/sub | solution.py:392
  70.9 0.0 copy-done.1
  70.9 1.4 %broadcast_multiply_fusion = f32[64,2048]{1,0:T(8,128)} fusion(f32[64,2048]{1,0:T(8,128)S(1)} %copy-done.1, f32[]{:T(128)} %bitcast.1), kind=kLoop, calls=%fused_computation | loop fusion | flops 131072 | bytes 1048580 | tf_op jit(solution)/shard_map/mul | solution.py:392
Async XLA Ops:
  0.6 68.3 %copy-start = (f32[64,2048]{1,0:T(8,128)S(1)}, f32[64,2048]{1,0:T(8,128)}, u32[]{:S(2)}) copy-start(f32[64,2048]{1,0:T(8,128)} %src_any.1) | copy-start | bytes 1572868
  68.9 2.0 %copy-start.1 = (f32[64,2048]{1,0:T(8,128)S(1)}, f32[64,2048]{1,0:T(8,128)}, u32[]{:S(2)}) copy-start(f32[64,2048]{1,0:T(8,128)} %get-tuple-element.8) | copy-start | bytes 1572868

commit v3 on v2

--- a/solution.py
+++ b/solution.py
@@ -56,11 +56,11 @@
 def kernel(
     doms, freqs, entries,
     v_ref, term_ref, cur_ref, chg_ref, high_any, low_any, src_any, jac_any,
-    back, raw_ref, norm_ref, scale_ref,
-    volt, seen, inc, partial, flow, stage, edge_out, edge, land, spec, high_ref, low_ref, src_ref,
+    out_any, norm_ref, scale_ref,
+    back, raw_ref, volt, seen, inc, partial, flow, stage, edge_out, edge, land, spec, high_ref, low_ref, src_ref,
     jac_ref, part_dom, part_freq,
     v_send, v_recv, edge_send, edge_recv, out_send, out_recv, back_send, back_recv,
-    pd_send, pd_recv, pf_send, pf_recv, load_sem,
+    pd_send, pd_recv, pf_send, pf_recv, load_sem, store_sem,
 ):
     dom = lax.axis_index("dom")
     freq = lax.axis_index("freq")
@@ -73,6 +73,7 @@
     pair = 2 * LANES
     ew = 512
     kb = 256
+    one, zero = jnp.bfloat16(1.0), jnp.bfloat16(0.0)
 
     barrier = pltpu.get_barrier_semaphore()
     for j in range(1, doms):
@@ -123,10 +124,11 @@
         first = jnp.where(same, -1, first)
         second = jnp.where(same, -1, second)
         total = jnp.zeros((2 * rows, ew), jnp.float32)
-        base = lax.broadcasted_iota(jnp.int32, (kb, ew), 0)
+        base = lax.broadcasted_iota(jnp.int16, (kb, ew), 0)
         for k in range(wide // kb):
-            tile = jnp.where(base == first - k * kb, 1.0, jnp.where(base == second - k * kb, -1.0, 0.0))
-            tile = tile.astype(jnp.bfloat16)
+            plus = base == (first - k * kb).astype(jnp.int16)
+            minus = base == (second - k * kb).astype(jnp.int16)
+            tile = jnp.where(plus, one, jnp.where(minus, -one, zero))
             inc[k * kb : (k + 1) * kb, cols] = tile
             if k * kb < nodes:
                 total = total + dot(volt[:, k * kb : (k + 1) * kb], tile)
@@ -176,10 +178,6 @@
             edge_out[i * per + c] = pieces[c]
         return carry
 
-    lax.fori_loop(0, (wide - nodes) // kb, border_block, 0)
-    for j in range(doms - 1, 0, -1):
-        edge_copy(j, xor(dom, j, doms), dom).start()
-
     my_rows = pl.ds(pl.multiple_of(freq * rows, rows), rows)
 
     def out_copy(c, j, sender):
@@ -194,8 +192,17 @@
         )
 
     def node_block(i, carry):
-        j = freqs - 1 - i
-        peer = xor(freq, j, freqs)
+        half = freqs // 2
+        far = (1 - freq // half) * half + half - 1 - i
+        peer = jnp.where(i < half, far, xor(freq, freqs - 1 - i, freqs))
+        j = xor(freq, peer, freqs)
+
+        @pl.when(i == 1)
+        def _():
+            lax.fori_loop(0, (wide - nodes) // kb, border_block, 0)
+            for k in range(doms - 1, 0, -1):
+                edge_copy(k, xor(dom, k, doms), dom).start()
+
         pieces = scatter(peer * block, block)
         for c in range(chunks):
             stage[c, peer] = pieces[c]
@@ -283,10 +290,17 @@
             upper = jnp.where(even, residual, pltpu.roll(residual, 1, 0))
             lower = jnp.where(even, pltpu.roll(residual, rows - 1, 0), residual)
             raw = -(jac_ref[:, 0, cols] * upper + jac_ref[:, 1, cols] * lower)
+            back[:, cols] = residual
             raw_ref[:, cols] = raw
             return carry[0] + fold(raw), carry[1] + fold(residual)
 
         sums = lax.fori_loop(0, freqs, finish, sums)
+
+    stores = [
+        pltpu.make_async_copy(a, out_any.at[i], store_sem.at[i]) for i, a in enumerate((back, raw_ref))
+    ]
+    for store in stores:
+        store.start()
 
     def whole(x):
         return jnp.sum(jnp.sum(x, axis=0, keepdims=True), axis=1, keepdims=True)
@@ -318,6 +332,8 @@
     spread = jnp.sqrt(raw_sum / entries + 1e-06)
     scale_ref[...] = jnp.minimum(1.0, trust_radius / spread)
     norm_ref[...] = jnp.sqrt(res_sum)
+    for store in stores:
+        store.wait()
 
     for j in range(1, doms):
         v_copy(j, dom).wait_send()
@@ -333,6 +349,11 @@
         return carry
 
     lax.fori_loop(0, freqs - 1, drain, 0)
+
+
+def damp_kernel(both_ref, scale_ref, residual_ref, step_ref):
+    residual_ref[...] = both_ref[0]
+    step_ref[...] = both_ref[1] * scale_ref[...]
 
 
 def body(doms, freqs, voltages, sources, terminals, elem_current, elem_charge, jacobi):
@@ -347,17 +368,18 @@
     vmem = pl.BlockSpec(memory_space=VMEM)
     anywhere = pl.BlockSpec(memory_space=pl.ANY)
     high, low = fourier_matrix(samples)
-    back, raw, norm, scale = pl.pallas_call(
+    both, norm, scale = pl.pallas_call(
         functools.partial(kernel, doms, freqs, float(samples * nodes * doms)),
         out_shape=(
-            jax.ShapeDtypeStruct((rows, nodes), f32),
-            jax.ShapeDtypeStruct((rows, nodes), f32),
+            jax.ShapeDtypeStruct((2, rows, nodes), f32),
             jax.ShapeDtypeStruct((1, 1), f32),
             jax.ShapeDtypeStruct((1, 1), f32),
         ),
         in_specs=[vmem] * 4 + [anywhere] * 4,
-        out_specs=(vmem,) * 4,
+        out_specs=(anywhere, vmem, vmem),
         scratch_shapes=[
+            VMEM((rows, nodes), f32),
+            VMEM((rows, nodes), f32),
             VMEM((2 * rows, wide), bf16),
             VMEM((doms, rows, border), f32),
             VMEM((wide, elems), bf16),
@@ -381,6 +403,7 @@
             dma((doms,)), dma((doms,)),
             dma((freqs,)), dma((freqs,)),
             dma((4,)),
+            dma((2,)),
         ],
         compiler_params=pltpu.CompilerParams(
             collective_id=0, has_side_effects=True, vmem_limit_bytes=60 * 1024 * 1024
@@ -389,7 +412,18 @@
         voltages, terminals, elem_current, elem_charge,
         jnp.asarray(high), jnp.asarray(low), sources, jacobi.reshape(rows, 2, nodes),
     )
-    return back - sources, raw * scale, norm.reshape(())
+    part = pl.BlockSpec((rows // 2, nodes), lambda i: (i, 0))
+    residual, step = pl.pallas_call(
+        damp_kernel,
+        grid=(2,),
+        out_shape=(jax.ShapeDtypeStruct((rows, nodes), f32),) * 2,
+        in_specs=[
+            pl.BlockSpec((2, rows // 2, nodes), lambda i: (0, i, 0)),
+            pl.BlockSpec((1, 1), lambda i: (0, 0)),
+        ],
+        out_specs=(part, part),
+    )(both, scale)
+    return residual, step, norm.reshape(())
 
 
 def solution(mesh):

time: 74.2 us -> 65.2 us (0.88)
  Pallas kernels: 68.3 us -> 62.6 us
  other arithmetic: 3.35 us -> 0 us
    pallas_call x1, Pallas kernels: 68.3 us -> 59.9 us  [body(): pl.pallas_call(functools.partial(kernel, doms, freqs, float(samples * nod...]
    pallas_call x0 -> x1, Pallas kernels: none -> 2.67 us  [body(): pl.pallas_call(damp_kernel, grid=(2,), out_shape=(jax.ShapeDtypeStruct((r...]
    sub x1 -> x0, other arithmetic: 1.95 us -> none  [body(): return (back - sources, raw * scale, norm.reshape(()))]
    mul x1 -> x0, other arithmetic: 1.4 us -> none  [body(): return (back - sources, raw * scale, norm.reshape(()))]
where the time goes in v3:
time: 65.2 us; the launch traced here: 65 us
  Pallas kernels  62.6 us (96%)
  between operations  2.4 us (4%)
    pallas_call x1, Pallas kernels, body(): pl.pallas_call(functools.partial(kernel, doms, freqs, float(samples * nod...  59.9 us
    pallas_call x1, Pallas kernels, body(): pl.pallas_call(damp_kernel, grid=(2,), out_shape=(jax.ShapeDtypeStruct((r...  2.67 us

profile of v3, /device:TPU:0, one launch (start us, length us, event | category | flops | bytes accessed | tf_op | source)
XLA Modules:
  0.0 65.0 jit_solution(14720605724187791104)
XLA Ops:
  0.6 59.9 %shard_map.103 = (f32[2,64,2048]{2,1,0:T(8,128)}, f32[1,1]{1,0:T(1,128)}, f32[1,1]{1,0:T(1,128)}) custom-call(f32[64,2048]{1,0:T(8,128)} %v_ref.1, s32[2,4096]{1,0:T(2,128)} %term_ref.1, f32[2,4096]{1,0:T(2,128)} %cur_ref.1, f32[2,4096]{1,0:T(2,128)} %chg_ref.1, bf16[512,512]{1,0:T(8,128)(2,1)} %constant.4.clone.high_any, ...), custom_call_target="tpu_custom_call" | custom-call | tf_op jit(solution)/shard_map/pallas_call | solution.py:371
  60.5 2.7 %shard_map.104 = (f32[64,2048]{1,0:T(8,128)}, f32[64,2048]{1,0:T(8,128)}) custom-call(f32[2,64,2048]{2,1,0:T(8,128)} %get-tuple-element.8.both_ref, f32[1,1]{1,0:T(1,128)} %get-tuple-element.9.scale_ref), custom_call_target="tpu_custom_call" | custom-call | tf_op jit(solution)/shard_map/pallas_call | solution.py:416

commit v4 on v3

--- a/solution.py
+++ b/solution.py
@@ -57,9 +57,9 @@
     doms, freqs, entries,
     v_ref, term_ref, cur_ref, chg_ref, high_any, low_any, src_any, jac_any,
     out_any, norm_ref, scale_ref,
-    back, raw_ref, volt, seen, inc, partial, flow, stage, edge_out, edge, land, spec, high_ref, low_ref, src_ref,
+    back, raw_ref, volt, seen, inc, partial, flow, stage, edge_out, edge, land, spec, mirror, joined, high_ref, low_ref, src_ref,
     jac_ref, part_dom, part_freq,
-    v_send, v_recv, edge_send, edge_recv, out_send, out_recv, back_send, back_recv,
+    v_send, v_recv, edge_send, edge_recv, out_send, out_recv, mirror_send, mirror_recv, back_send, back_recv,
     pd_send, pd_recv, pf_send, pf_recv, load_sem, store_sem,
 ):
     dom = lax.axis_index("dom")
@@ -68,9 +68,12 @@
     wide, elems = inc.shape
     border = seen.shape[2]
     samples = rows * freqs
-    block = nodes // freqs
-    chunks = block // LANES
-    pair = 2 * LANES
+    near = freqs // 2
+    half = freq // near
+    mine = freq % near
+    mirror_id = freq + near * (1 - 2 * half)
+    group = nodes // near
+    chunks = group // LANES
     ew = 512
     kb = 256
     one, zero = jnp.bfloat16(1.0), jnp.bfloat16(0.0)
@@ -178,73 +181,84 @@
             edge_out[i * per + c] = pieces[c]
         return carry
 
-    my_rows = pl.ds(pl.multiple_of(freq * rows, rows), rows)
+    def peer_of(j):
+        return xor(mine, j, near)
+
+    def piece(index):
+        return pl.ds(pl.multiple_of(index * rows, rows), rows)
 
     def out_copy(c, j, sender):
-        peer = xor(freq, j, freqs)
+        peer = peer_of(j)
         return pltpu.make_async_remote_copy(
             src_ref=stage.at[c, peer],
-            dst_ref=land.at[c, pl.ds(pl.multiple_of(sender * rows, rows), rows), :],
+            dst_ref=land.at[c, piece(sender), :],
             send_sem=out_send.at[c, j],
             recv_sem=out_recv.at[c, sender],
-            device_id={"freq": peer},
+            device_id={"freq": half * near + peer},
             device_id_type=MESH,
         )
 
-    def node_block(i, carry):
-        half = freqs // 2
-        far = (1 - freq // half) * half + half - 1 - i
-        peer = jnp.where(i < half, far, xor(freq, freqs - 1 - i, freqs))
-        j = xor(freq, peer, freqs)
-
-        @pl.when(i == 1)
-        def _():
-            lax.fori_loop(0, (wide - nodes) // kb, border_block, 0)
-            for k in range(doms - 1, 0, -1):
-                edge_copy(k, xor(dom, k, doms), dom).start()
-
-        pieces = scatter(peer * block, block)
-        for c in range(chunks):
-            stage[c, peer] = pieces[c]
-
-        @pl.when(peer == 0)
-        def _():
-            for k in range(1, doms):
-                edge_copy(k, dom, xor(dom, k, doms)).wait_recv()
-            total = stage[0, 0] + edge_out[dom]
-            for p in range(doms):
-                total = total + jnp.where(dom == p, 0.0, edge[p])
-            stage[0, 0] = total
-
-        @pl.when(j != 0)
-        def _():
-            out_copy(0, j, freq).start()
-
-        return carry
-
-    lax.fori_loop(0, freqs, node_block, 0)
-
-    def later(i, carry):
-        for c in range(1, chunks):
-            out_copy(c, freqs - 1 - i, freq).start()
-        return carry
-
-    if chunks > 1:
-        lax.fori_loop(0, freqs - 1, later, 0)
-
-    for c in range(chunks):
-        land[c, my_rows, :] = stage[c, freq]
+    order = []
+    for b in range(group // kb - 1, -1, -1):
+        order += [b * per + c for c in range(per)]
+
+        def node_block(i, carry):
+            peer = near - 1 - i
+            j = xor(mine, peer, near)
+            if b == group // kb - 1:
+                @pl.when(i == 1)
+                def _():
+                    lax.fori_loop(0, (wide - nodes) // kb, border_block, 0)
+                    for k in range(doms - 1, 0, -1):
+                        edge_copy(k, xor(dom, k, doms), dom).start()
+
+            pieces = scatter(peer * group + b * kb, kb)
+            for c in range(per):
+                stage[b * per + c, peer] = pieces[c]
+            if b == 0:
+                @pl.when(peer == 0)
+                def _():
+                    for k in range(1, doms):
+                        edge_copy(k, dom, xor(dom, k, doms)).wait_recv()
+                    total = stage[0, 0] + edge_out[dom]
+                    for p in range(doms):
+                        total = total + jnp.where(dom == p, 0.0, edge[p])
+                    stage[0, 0] = total
+
+            @pl.when(j != 0)
+            def _():
+                for c in range(per):
+                    out_copy(b * per + c, j, mine).start()
+
+            return carry
+
+        lax.fori_loop(0, near, node_block, 0)
 
     def back_columns(c, sender):
         return pl.ds(pl.multiple_of((sender * chunks + c) * LANES, LANES), LANES)
 
     def back_copy(c, j, target, sender):
         return pltpu.make_async_remote_copy(
-            src_ref=spec.at[c, pl.ds(pl.multiple_of(target * rows, rows), rows), :],
+            src_ref=joined.at[c, piece(target), :],
             dst_ref=back.at[:, back_columns(c, sender)],
             send_sem=back_send.at[c, j],
             recv_sem=back_recv.at[c, sender],
-            device_id={"freq": xor(freq, j, freqs)},
+            device_id={"freq": half * near + peer_of(j)},
+            device_id_type=MESH,
+        )
+
+    span = near * rows
+
+    def half_rows(which):
+        return pl.ds(pl.multiple_of(which * span, span), span)
+
+    def mirror_copy(c):
+        return pltpu.make_async_remote_copy(
+            src_ref=spec.at[c, half_rows(1 - half), :],
+            dst_ref=mirror.at[c],
+            send_sem=mirror_send.at[c],
+            recv_sem=mirror_recv.at[c],
+            device_id={"freq": mirror_id},
             device_id_type=MESH,
         )
 
@@ -253,23 +267,38 @@
     row = lax.broadcasted_iota(jnp.int32, (samples, LANES), 0)
     rate = (row // 2).astype(jnp.float32) * (2.0 / samples)
     rate = jnp.where(row % 2 == 0, rate, -rate)
-    for c in range(chunks):
+
+    def transform(c):
+        land[c, piece(mine), :] = stage[c, mine]
+
         def arrived(i, carry):
-            out_copy(c, freqs - 1 - i, xor(freq, freqs - 1 - i, freqs)).wait_recv()
+            out_copy(c, near - 1 - i, peer_of(near - 1 - i)).wait_recv()
             return carry
 
-        lax.fori_loop(0, freqs - 1, arrived, 0)
+        lax.fori_loop(0, near - 1, arrived, 0)
         high, low = split(land[c])
-        product = dot(high_ref[...], high) + (dot(high_ref[...], low) + dot(low_ref[...], high))
+        big = high_ref[:, half_rows(half)]
+        product = dot(big, high) + (dot(big, low) + dot(low_ref[:, half_rows(half)], high))
         spec[c] = product[:, :LANES] + rate * swap_pairs(product[:, LANES:])
+        mirror_copy(c).start()
+
+    def join(c):
+        mirror_copy(c).wait_recv()
+        joined[c] = spec[c, half_rows(half), :] + mirror[c]
 
         def give(i, carry):
-            j = freqs - 1 - i
-            back_copy(c, j, xor(freq, j, freqs), freq).start()
+            j = near - 1 - i
+            back_copy(c, j, peer_of(j), mine).start()
             return carry
 
-        lax.fori_loop(0, freqs - 1, give, 0)
-        back[:, back_columns(c, freq)] = spec[c, my_rows, :]
+        lax.fori_loop(0, near - 1, give, 0)
+        back[:, back_columns(c, mine)] = joined[c, piece(mine), :]
+
+    for i, c in enumerate(order):
+        transform(c)
+        if i:
+            join(order[i - 1])
+    join(order[-1])
 
     even = lax.broadcasted_iota(jnp.int32, (rows, LANES), 0) % 2 == 0
     sums = (jnp.zeros((8, LANES), jnp.float32), jnp.zeros((8, LANES), jnp.float32))
@@ -277,9 +306,9 @@
     def fold(x):
         return jnp.sum((x * x).reshape(rows // 8, 8, LANES), axis=0)
 
-    for c in range(chunks):
+    for c in order:
         def finish(j, carry):
-            peer = xor(freq, j, freqs)
+            peer = peer_of(j)
 
             @pl.when(j != 0)
             def _():
@@ -294,7 +323,7 @@
             raw_ref[:, cols] = raw
             return carry[0] + fold(raw), carry[1] + fold(residual)
 
-        sums = lax.fori_loop(0, freqs, finish, sums)
+        sums = lax.fori_loop(0, near, finish, sums)
 
     stores = [
         pltpu.make_async_copy(a, out_any.at[i], store_sem.at[i]) for i, a in enumerate((back, raw_ref))
@@ -340,15 +369,23 @@
         edge_copy(j, dom, dom).wait_send()
         part_copy("dom", doms, dom, part_dom, pd_send, pd_recv, j, dom).wait_send()
 
+    for c in range(chunks):
+        mirror_copy(c).wait_send()
+
     def drain(i, carry):
         j = i + 1
         for c in range(chunks):
-            out_copy(c, j, freq).wait_send()
-            back_copy(c, j, freq, freq).wait_send()
-        part_copy("freq", freqs, freq, part_freq, pf_send, pf_recv, j, freq).wait_send()
+            out_copy(c, j, mine).wait_send()
+            back_copy(c, j, mine, mine).wait_send()
         return carry
 
-    lax.fori_loop(0, freqs - 1, drain, 0)
+    lax.fori_loop(0, near - 1, drain, 0)
+
+    def drain_parts(i, carry):
+        part_copy("freq", freqs, freq, part_freq, pf_send, pf_recv, i + 1, freq).wait_send()
+        return carry
+
+    lax.fori_loop(0, freqs - 1, drain_parts, 0)
 
 
 def damp_kernel(both_ref, scale_ref, residual_ref, step_ref):
@@ -362,7 +399,8 @@
     border = nodes // 16
     wide = nodes + doms * border
     samples = rows * freqs
-    chunks = nodes // freqs // LANES
+    near = freqs // 2
+    chunks = nodes // near // LANES
     f32, bf16 = jnp.float32, jnp.bfloat16
     dma = pltpu.SemaphoreType.DMA
     vmem = pl.BlockSpec(memory_space=VMEM)
@@ -385,11 +423,13 @@
             VMEM((wide, elems), bf16),
             VMEM((rows, elems), f32),
             VMEM((4 * rows, elems), bf16),
-            VMEM((chunks, freqs, rows, 2 * LANES), f32),
+            VMEM((chunks, near, rows, 2 * LANES), f32),
             VMEM((doms, rows, 2 * LANES), f32),
             VMEM((doms, rows, 2 * LANES), f32),
-            VMEM((chunks, samples, 2 * LANES), f32),
+            VMEM((chunks, near * rows, 2 * LANES), f32),
             VMEM((chunks, samples, LANES), f32),
+            VMEM((chunks, near * rows, LANES), f32),
+            VMEM((chunks, near * rows, LANES), f32),
             VMEM((samples, samples), bf16),
             VMEM((samples, samples), bf16),
             VMEM((rows, nodes), f32),
@@ -398,8 +438,9 @@
             VMEM((freqs, 8, LANES), f32),
             dma((doms,)), dma((doms,)),
             dma((doms,)), dma((doms,)),
-            dma((chunks, freqs)), dma((chunks, freqs)),
-            dma((chunks, freqs)), dma((chunks, freqs)),
+            dma((chunks, near)), dma((chunks, near)),
+            dma((chunks,)), dma((chunks,)),
+            dma((chunks, near)), dma((chunks, near)),
             dma((doms,)), dma((doms,)),
             dma((freqs,)), dma((freqs,)),
             dma((4,)),

time: 65.2 us -> 65.3 us (level)
  no operation moved by 1% of the time
where the time goes in v4:
time: 65.3 us; the launch traced here: 65.1 us
  Pallas kernels  62.7 us (96%)
  between operations  2.4 us (4%)
    pallas_call x1, Pallas kernels, body(): pl.pallas_call(functools.partial(kernel, doms, freqs, float(samples * nod...  60.1 us
    pallas_call x1, Pallas kernels, body(): pl.pallas_call(damp_kernel, grid=(2,), out_shape=(jax.ShapeDtypeStruct((r...  2.67 us

profile of v4, /device:TPU:0, one launch (start us, length us, event | category | flops | bytes accessed | tf_op | source)
XLA Modules:
  0.0 65.1 jit_solution(14390422506714119566)
XLA Ops:
  0.6 60.1 %shard_map.103 = (f32[2,64,2048]{2,1,0:T(8,128)}, f32[1,1]{1,0:T(1,128)}, f32[1,1]{1,0:T(1,128)}) custom-call(f32[64,2048]{1,0:T(8,128)} %v_ref.1, s32[2,4096]{1,0:T(2,128)} %term_ref.1, f32[2,4096]{1,0:T(2,128)} %cur_ref.1, f32[2,4096]{1,0:T(2,128)} %chg_ref.1, bf16[512,512]{1,0:T(8,128)(2,1)} %constant.4.clone.high_any, ...), custom_call_target="tpu_custom_call" | custom-call | tf_op jit(solution)/shard_map/pallas_call | solution.py:409
  60.7 2.7 %shard_map.104 = (f32[64,2048]{1,0:T(8,128)}, f32[64,2048]{1,0:T(8,128)}) custom-call(f32[2,64,2048]{2,1,0:T(8,128)} %get-tuple-element.8.both_ref, f32[1,1]{1,0:T(1,128)} %get-tuple-element.9.scale_ref), custom_call_target="tpu_custom_call" | custom-call | tf_op jit(solution)/shard_map/pallas_call | solution.py:457

commit v5 on v4

--- a/solution.py
+++ b/solution.py
@@ -198,6 +198,66 @@
             device_id_type=MESH,
         )
 
+    def back_columns(c, sender):
+        return pl.ds(pl.multiple_of((sender * chunks + c) * LANES, LANES), LANES)
+
+    def back_copy(c, j, target, sender):
+        return pltpu.make_async_remote_copy(
+            src_ref=joined.at[c, piece(target), :],
+            dst_ref=back.at[:, back_columns(c, sender)],
+            send_sem=back_send.at[c, j],
+            recv_sem=back_recv.at[c, sender],
+            device_id={"freq": half * near + peer_of(j)},
+            device_id_type=MESH,
+        )
+
+    span = near * rows
+
+    def half_rows(which):
+        return pl.ds(pl.multiple_of(which * span, span), span)
+
+    def mirror_copy(c):
+        return pltpu.make_async_remote_copy(
+            src_ref=spec.at[c, half_rows(1 - half), :],
+            dst_ref=mirror.at[c],
+            send_sem=mirror_send.at[c],
+            recv_sem=mirror_recv.at[c],
+            device_id={"freq": mirror_id},
+            device_id_type=MESH,
+        )
+
+    for load in loads:
+        load.wait()
+    row = lax.broadcasted_iota(jnp.int32, (samples, LANES), 0)
+    rate = (row // 2).astype(jnp.float32) * (2.0 / samples)
+    rate = jnp.where(row % 2 == 0, rate, -rate)
+
+    def transform(c):
+        land[c, piece(mine), :] = stage[c, mine]
+
+        def arrived(i, carry):
+            out_copy(c, near - 1 - i, peer_of(near - 1 - i)).wait_recv()
+            return carry
+
+        lax.fori_loop(0, near - 1, arrived, 0)
+        high, low = split(land[c])
+        big = high_ref[:, half_rows(half)]
+        product = dot(big, high) + (dot(big, low) + dot(low_ref[:, half_rows(half)], high))
+        spec[c] = product[:, :LANES] + rate * swap_pairs(product[:, LANES:])
+        mirror_copy(c).start()
+
+    def join(c):
+        mirror_copy(c).wait_recv()
+        joined[c] = spec[c, half_rows(half), :] + mirror[c]
+
+        def give(i, carry):
+            j = near - 1 - i
+            back_copy(c, j, peer_of(j), mine).start()
+            return carry
+
+        lax.fori_loop(0, near - 1, give, 0)
+        back[:, back_columns(c, mine)] = joined[c, piece(mine), :]
+
     order = []
     for b in range(group // kb - 1, -1, -1):
         order += [b * per + c for c in range(per)]
@@ -232,73 +292,20 @@
 
             return carry
 
-        lax.fori_loop(0, near, node_block, 0)
-
-    def back_columns(c, sender):
-        return pl.ds(pl.multiple_of((sender * chunks + c) * LANES, LANES), LANES)
-
-    def back_copy(c, j, target, sender):
-        return pltpu.make_async_remote_copy(
-            src_ref=joined.at[c, piece(target), :],
-            dst_ref=back.at[:, back_columns(c, sender)],
-            send_sem=back_send.at[c, j],
-            recv_sem=back_recv.at[c, sender],
-            device_id={"freq": half * near + peer_of(j)},
-            device_id_type=MESH,
-        )
-
-    span = near * rows
-
-    def half_rows(which):
-        return pl.ds(pl.multiple_of(which * span, span), span)
-
-    def mirror_copy(c):
-        return pltpu.make_async_remote_copy(
-            src_ref=spec.at[c, half_rows(1 - half), :],
-            dst_ref=mirror.at[c],
-            send_sem=mirror_send.at[c],
-            recv_sem=mirror_recv.at[c],
-            device_id={"freq": mirror_id},
-            device_id_type=MESH,
-        )
-
-    for load in loads:
-        load.wait()
-    row = lax.broadcasted_iota(jnp.int32, (samples, LANES), 0)
-    rate = (row // 2).astype(jnp.float32) * (2.0 / samples)
-    rate = jnp.where(row % 2 == 0, rate, -rate)
-
-    def transform(c):
-        land[c, piece(mine), :] = stage[c, mine]
-
-        def arrived(i, carry):
-            out_copy(c, near - 1 - i, peer_of(near - 1 - i)).wait_recv()
-            return carry
-
-        lax.fori_loop(0, near - 1, arrived, 0)
-        high, low = split(land[c])
-        big = high_ref[:, half_rows(half)]
-        product = dot(big, high) + (dot(big, low) + dot(low_ref[:, half_rows(half)], high))
-        spec[c] = product[:, :LANES] + rate * swap_pairs(product[:, LANES:])
-        mirror_copy(c).start()
-
-    def join(c):
-        mirror_copy(c).wait_recv()
-        joined[c] = spec[c, half_rows(half), :] + mirror[c]
-
-        def give(i, carry):
-            j = near - 1 - i
-            back_copy(c, j, peer_of(j), mine).start()
-            return carry
-
-        lax.fori_loop(0, near - 1, give, 0)
-        back[:, back_columns(c, mine)] = joined[c, piece(mine), :]
-
-    for i, c in enumerate(order):
+        early = order[:-per] if b == 0 else []
+        lax.fori_loop(0, near // 2, node_block, 0)
+        for c in early:
+            transform(c)
+        lax.fori_loop(near // 2, near, node_block, 0)
+
+    waiting = order[:-per]
+    for c in order[-per:]:
+        if waiting:
+            join(waiting.pop(0))
         transform(c)
-        if i:
-            join(order[i - 1])
-    join(order[-1])
+        waiting.append(c)
+    for c in waiting:
+        join(c)
 
     even = lax.broadcasted_iota(jnp.int32, (rows, LANES), 0) % 2 == 0
     sums = (jnp.zeros((8, LANES), jnp.float32), jnp.zeros((8, LANES), jnp.float32))

time: 65.3 us -> 63.6 us (0.974)
  Pallas kernels: 62.7 us -> 61 us
    pallas_call x1, Pallas kernels: 60.1 us -> 58.4 us  [body(): pl.pallas_call(functools.partial(kernel, doms, freqs, float(samples * nod...]
where the time goes in v5:
time: 63.6 us; the launch traced here: 63.4 us
  Pallas kernels  61 us (96%)
  between operations  2.4 us (4%)
    pallas_call x1, Pallas kernels, body(): pl.pallas_call(functools.partial(kernel, doms, freqs, float(samples * nod...  58.4 us
    pallas_call x1, Pallas kernels, body(): pl.pallas_call(damp_kernel, grid=(2,), out_shape=(jax.ShapeDtypeStruct((r...  2.67 us

profile of v5, /device:TPU:0, one launch (start us, length us, event | category | flops | bytes accessed | tf_op | source)
XLA Modules:
  0.0 63.4 jit_solution(16983274497529489938)
XLA Ops:
  0.6 58.4 %shard_map.103 = (f32[2,64,2048]{2,1,0:T(8,128)}, f32[1,1]{1,0:T(1,128)}, f32[1,1]{1,0:T(1,128)}) custom-call(f32[64,2048]{1,0:T(8,128)} %v_ref.1, s32[2,4096]{1,0:T(2,128)} %term_ref.1, f32[2,4096]{1,0:T(2,128)} %cur_ref.1, f32[2,4096]{1,0:T(2,128)} %chg_ref.1, bf16[512,512]{1,0:T(8,128)(2,1)} %constant.4.clone.high_any, ...), custom_call_target="tpu_custom_call" | custom-call | tf_op jit(solution)/shard_map/pallas_call | solution.py:416
  59.0 2.7 %shard_map.104 = (f32[64,2048]{1,0:T(8,128)}, f32[64,2048]{1,0:T(8,128)}) custom-call(f32[2,64,2048]{2,1,0:T(8,128)} %get-tuple-element.8.both_ref, f32[1,1]{1,0:T(1,128)} %get-tuple-element.9.scale_ref), custom_call_target="tpu_custom_call" | custom-call | tf_op jit(solution)/shard_map/pallas_call | solution.py:464
